TPU v7x, 32 devices: a whole 2x2x4 slice. The times are simulated.
32 devices in a mesh: hi: 4 (over x, core), lo: 8 (over z, y).
Axes of the slice: x: 2, y: 2, z: 4, core: 2. Of those that a mesh axis runs over, the one named last changes fastest.
Arguments:
- current: float32 [131072, 256], P(('hi', 'lo')), may hold values from -130 to 130
- signs: int32 [131072], P(('hi', 'lo')), may hold values from -1 to 1, as said below
- sample_rows: int32 [512], P(('hi', 'lo')), may hold values from 0 to 4095
- sample_owner: int32 [512, 1], P(('hi', 'lo')), may hold values from 0 to 7; in each aligned block of 16 rows (0 to 15, 16 to 31, ...) at most 2 rows name the same one
Outputs:
- sketch: float32 [4, 8, 8, 2, 256], P('hi', 'lo')
- r_factor: float32 [256, 256], replicated
- precond: float32 [131072, 256], P(('hi', 'lo'))
Inputs may be any that keep to these rules, and one draw needn't show every extreme that they name: `signs`: each entry is -1 or 1. `sample_owner`: among the 16 samples of one device no owner is named more than 2 times, and in every draw some device names some owner exactly 2 times.
All inputs are finite; a program needn't handle non-finite values.
Results may differ from a plain program's by a relative error of at most 0.000098.
Values sent between devices are 32-bit elements; how exact they have to be, the bound alone decides.
A program may use at most 64 MiB of HBM per device.

v0:
```python
import math
import jax
import jax.numpy as jnp
from jax import lax
from jax.sharding import PartitionSpec as P

MOST = 2
HIGHEST = lax.Precision.HIGHEST


def sylvester(order_size):
    hadamard_table = jnp.ones((1, 1), jnp.float32)
    base_pair = jnp.array([[1.0, 1.0], [1.0, -1.0]], jnp.float32)
    while hadamard_table.shape[0] < order_size:
        hadamard_table = jnp.kron(hadamard_table, base_pair)
    return hadamard_table


def split_order(order_size):
    leading = 2 ** ((order_size.bit_length() - 1) // 2)
    return (leading, order_size // leading)


def shards(current, signs, sample_rows, sample_owner):
    rows_here = current.shape[0]
    panel_width = current.shape[1]
    high_count = lax.axis_size("hi")
    low_count = lax.axis_size("lo")
    devices = high_count * low_count
    count_here = sample_rows.shape[0]
    scale_all = 1.0 / math.sqrt(rows_here * devices)
    signed = current * signs.astype(jnp.float32)[:, None]
    leading, second = split_order(rows_here)
    shaped = signed.reshape(leading, second, panel_width)
    shaped = jnp.einsum("ab,bcp->acp", sylvester(leading), shaped, precision=HIGHEST)
    shaped = jnp.einsum("cd,adp->acp", sylvester(second), shaped, precision=HIGHEST)
    mixture = shaped.reshape(rows_here, panel_width)
    all_samples = lax.all_gather(sample_rows, ("hi", "lo"), axis=0, tiled=True)
    own_device = lax.axis_index("hi") * low_count + lax.axis_index("lo")
    column_signs = lax.dynamic_index_in_dim(sylvester(devices), own_device, 1, keepdims=False)
    row_signs = jnp.repeat(column_signs, count_here)
    shares = jnp.take(mixture, all_samples, axis=0) * row_signs[:, None]
    picked = lax.psum_scatter(shares, ("hi", "lo"), scatter_dimension=0, tiled=True) * scale_all
    owner_ids = sample_owner[:, 0]
    owner_hot = (owner_ids[:, None] == jnp.arange(low_count, dtype=jnp.int32)[None, :]).astype(
        jnp.int32
    )
    before = jnp.cumsum(owner_hot, axis=0) - owner_hot
    slot_ids = jnp.sum(before * owner_hot, axis=1)
    placement = (owner_hot.T[:, None, :] == 1) & (
        slot_ids[None, None, :] == jnp.arange(MOST, dtype=jnp.int32)[None, :, None]
    )
    outgoing = jnp.einsum("omk,kp->omp", placement.astype(jnp.float32), picked, precision=HIGHEST)
    received = lax.all_to_all(outgoing, "lo", split_axis=0, concat_axis=0, tiled=True)
    sketch = received.reshape(1, 1, low_count, MOST, panel_width)
    owned_rows = received.reshape(low_count * MOST, panel_width)
    local_gram = jnp.dot(owned_rows.T, owned_rows, precision=HIGHEST)
    gram_total = lax.psum(local_gram, ("hi", "lo")) * (1.0 / (count_here * devices))
    lower_factor = jnp.linalg.cholesky(gram_total)
    precond = lax.linalg.triangular_solve(
        lower_factor, current, left_side=False, lower=True, transpose_a=True
    )
    return (sketch, lower_factor.T, precond)


def solution(mesh):
    placed = (P(("hi", "lo"), None), P(("hi", "lo")), P(("hi", "lo")), P(("hi", "lo"), None))
    return jax.shard_map(
        shards,
        mesh=mesh,
        in_specs=placed,
        out_specs=(P("hi", "lo", None, None, None), P(), P(("hi", "lo"), None)),
        check_vma=False,
    )
```

profile of v0, /device:TPU:0, one launch (start us, length us, event | category | flops | bytes accessed | tf_op | source)
XLA Modules:
  0.0 434.3 jit_solution(16142233087019374915)
XLA Ops:
  7.2 0.9 dynamic-update-slice.11
  8.1 42.0 %all-reduce.1 = s32[512]{0:T(512)S(1)} all-reduce(s32[512]{0:T(512)S(1)} %dynamic-update-slice.11), channel_id=1, replica_groups=mesh['hi'=4,'lo'=8] {'hi','lo'}, use_global_device_ids=true, to_apply=%add.1 | all-reduce | flops 512 | bytes 4096
  50.1 0.8 broadcast_multiply_fusion.6
  50.9 0.1 mul.371
  51.0 0.8 broadcast_multiply_fusion.5
  51.8 0.1 mul.375
  51.8 0.7 convert_element_type.16
  52.6 0.8 broadcast_multiply_fusion.4
  53.3 0.1 mul.379
  53.4 0.8 broadcast_multiply_fusion.3
  54.2 0.1 mul.383
  54.3 0.9 broadcast_multiply_fusion.1
  55.2 0.2 dynamic-slice_reduce_fusion
  55.5 0.1 mul.427
  55.6 0.7 reshape.344
  56.2 2.6 broadcast_multiply_fusion
  58.8 6.3 %fusion.2 = f32[64,64,256]{2,0,1:T(8,128)S(1)} fusion(f32[64,64,1]{1,0,2:T(8,128)S(1)} %reshape.344, f32[64,64,256]{2,1,0:T(8,128)S(1)} %bitcast.55), kind=kOutput, calls=%fused_computation.7 | convolution fusion | flops 805306368 | bytes 8404992 | tf_op jit(solution)/shard_map/ab,bcp->acp/dot_general | solution.py:35
  65.1 7.0 %fusion = f32[64,256,64]{1,2,0:T(8,128)} fusion(f32[64,64,1]{1,0,2:T(8,128)S(1)} %reshape.344, f32[64,64,256]{2,0,1:T(8,128)S(1)} %fusion.2), kind=kOutput, calls=%fused_computation.5 | convolution fusion | flops 805306368 | bytes 8404992 | tf_op jit(solution)/shard_map/cd,adp->acp/dot_general | solution.py:36
  72.2 3.8 gather_fusion
  75.9 1.0 select_multiply_fusion
  77.1 0.2 select_reduce_fusion.2
  77.3 135.4 %reduce-scatter.2.cloned.1.call-done = f32[16,256]{1,0:T(8,128)} async-done(((f32[512,256]{1,0:T(8,128)}), f32[16,256]{1,0:T(8,128)}) %reduce-scatter.2.cloned.1.call-update) | async-done | bytes 16400 | tf_op jit(solution)/shard_map/reduce_scatter | solution.py:43
  212.7 0.8 fusion.14
  213.6 8.9 %all_to_all.5 = f32[8,2,256]{2,1,0:T(2,128)S(1)} all-to-all(f32[8,2,256]{2,1,0:T(2,128)S(1)} %copy.33), channel_id=1, replica_groups=mesh['hi'=4,'lo'=8] {'lo'}, dimensions={0} | all-to-all | bytes 32768 | tf_op jit(solution)/shard_map/all_to_all | solution.py:54
  222.5 1.1 convolution_bitcast_fusion
  223.7 123.2 %all-reduce.4.cloned.1.call-done = f32[256,256]{0,1:T(8,128)} async-done(((f32[256,256]{0,1:T(8,128)}), f32[256,256]{0,1:T(8,128)}) %all-reduce.4.cloned.1.call-update) | async-done | bytes 262160 | tf_op jit(solution)/shard_map/psum | solution.py:58
  346.9 1.0 broadcast_multiply_fusion.2
  347.8 0.1 copy.37
  348.0 1.0 fusion.6
  349.0 11.7 %cholesky.50 = f32[128,128]{1,0:T(8,128)S(1)} custom-call(f32[128,128]{1,0:T(8,128)S(1)} %cholesky.118), custom_call_target="Cholesky" | custom-call | tf_op jit(solution)/shard_map/jit(cholesky)/cholesky | solution.py:59
  360.7 9.8 %custom-call.14 = f32[1,128,128]{1,2,0:T(8,128)S(1)} custom-call(f32[1,128,128]{2,1,0:T(8,128)S(1)} %get-tuple-element.38), custom_call_target="InvertDiagBlocksLowerTriangular" | custom-call | tf_op jit(solution)/shard_map/jit(cholesky)/cholesky | solution.py:59
  370.6 0.2 constant_dynamic-update-slice_fusion.1
  370.8 0.3 convolution_subtract_fusion.1
  371.0 11.7 %cholesky.105 = f32[128,128]{1,0:T(8,128)S(1)} custom-call(f32[128,128]{1,0:T(8,128)S(1)} %convolution_subtract_fusion.1), custom_call_target="Cholesky" | custom-call | tf_op jit(solution)/shard_map/jit(cholesky)/cholesky | solution.py:59
  382.8 0.6 compare_reduce_fusion
  384.8 0.8 copy.38
  385.7 4.1 while.1
  385.7 0.6 fusion.32
  386.3 1.4 bitcast_dynamic-update-slice_fusion.2
  387.7 0.6 fusion.32
  388.3 1.4 bitcast_dynamic-update-slice_fusion.2
  389.8 19.9 %custom-call.15 = f32[2,128,128]{1,2,0:T(8,128)S(1)} custom-call(f32[2,128,128]{2,1,0:T(8,128)S(1)} %get-tuple-element.10), custom_call_target="InvertDiagBlocksLowerTriangular" | custom-call | tf_op jit(solution)/shard_map/triangular_solve | solution.py:60
  409.7 3.7 fusion.4
  413.4 3.4 convolution_subtract_fusion
  416.8 2.0 fusion.9
  418.9 2.4 pad_maximum_fusion
  421.3 5.6 %copy.39 = f32[4096,256]{1,0:T(8,128)} copy(f32[4096,256]{0,1:T(8,128)} %pad_maximum_fusion) | data formatting | bytes 8388608
  426.8 0.6 copy.62
  (28 shorter events, 0.6 us)
Async XLA Ops:
  7.2 205.6 %reduce-scatter.2.cloned.1.call-start = ((), (), s32[]{:S(2)}) async-start(), calls=%async_computation.2 | async-start | bytes 540672 | tf_op jit(solution)/shard_map/reduce_scatter | solution.py:43
  72.2 4.9 %copy-start.1 = (s32[16,1]{0,1:T(1,128)S(1)}, s32[16,1]{0,1:T(1,128)}, u32[]{:S(2)}) copy-start(s32[16,1]{0,1:T(1,128)} %param.10) | copy-start | bytes 196
  77.0 269.9 %all-reduce.4.cloned.1.call-start = ((), (), s32[]{:S(2)}) async-start(), calls=%async_computation.3 | async-start | bytes 524288 | tf_op jit(solution)/shard_map/psum | solution.py:58
  409.7 3.7 copy-start
Sparse Core Ops, SparseCore 0:
  77.1 135.6 reduce-scatter.1
  223.8 123.0 all-reduce.3
where the time goes:
time: 435 us; the launch traced here: 434 us
  waiting for transfers between devices  259 us (60%)
  other arithmetic  66.9 us (15%)
  blocking collectives  50.9 us (12%)
  matrix products  24.9 us (6%)
  local copies, waits for them, and re-layouts  17.4 us (4%)
  between operations  15.6 us (4%)
    reduce_scatter x1, waiting for transfers between devices, shards(): lax.psum_scatter(shares, ('hi', 'lo'), scatter_dimension=0, tiled=True)  135 us
    psum x1, waiting for transfers between devices, shards(): lax.psum(local_gram, ('hi', 'lo')) * (1.0 / (count_here * devices))  123 us
    unnamed x1, blocking collectives  42 us
    another operation x6, other arithmetic, shards(): lower_factor = jnp.linalg.cholesky(gram_total)  34 us
    another operation x4, other arithmetic, shards(): lax.linalg.triangular_solve(lower_factor, current, left_side=False, lower...  22.3 us
    another operation x3, matrix products, shards(): lax.linalg.triangular_solve(lower_factor, current, left_side=False, lower...  9.13 us
    all_to_all x1, blocking collectives, shards(): lax.all_to_all(outgoing, 'lo', split_axis=0, concat_axis=0, tiled=True)  8.94 us
  transfers between devices with their start and end apart: 2, of which 2 were waited for; matrix products, arithmetic and copies ran while one was open for 0% of the time, Pallas kernels for 0%

commit v1 on v0

--- a/solution.py
+++ b/solution.py
@@ -55,7 +55,7 @@
     sketch = received.reshape(1, 1, low_count, MOST, panel_width)
     owned_rows = received.reshape(low_count * MOST, panel_width)
     local_gram = jnp.dot(owned_rows.T, owned_rows, precision=HIGHEST)
-    gram_total = lax.psum(local_gram, ("hi", "lo")) * (1.0 / (count_here * devices))
+    gram_total = lax.psum(lax.psum(local_gram, "lo"), "hi") * (1.0 / (count_here * devices))
     lower_factor = jnp.linalg.cholesky(gram_total)
     precond = lax.linalg.triangular_solve(
         lower_factor, current, left_side=False, lower=True, transpose_a=True

time: 435 us -> 413 us (0.949)
  waiting for transfers between devices: 259 us -> 237 us
    psum x1 -> x2, waiting for transfers between devices: 123 us -> 101 us  [the longest x1 67.5 us: shards(): lax.psum(local_gram, 'lo')]
  transfers between devices with their start and end apart: 2 -> 3, of which waited for: 2 -> 3; matrix products, arithmetic and copies ran while one was open for 0% -> 0% of each run, Pallas kernels for 0% -> 0%
where the time goes in v1:
time: 413 us; the launch traced here: 412 us
  waiting for transfers between devices  237 us (57%)
  other arithmetic  66.7 us (16%)
  blocking collectives  50.9 us (12%)
  matrix products  24.9 us (6%)
  local copies, waits for them, and re-layouts  17.4 us (4%)
  between operations  15.3 us (4%)
    reduce_scatter x1, waiting for transfers between devices, shards(): lax.psum_scatter(shares, ('hi', 'lo'), scatter_dimension=0, tiled=True)  135 us
    psum x1, waiting for transfers between devices, shards(): lax.psum(local_gram, 'lo')  67.5 us
    unnamed x1, blocking collectives  42 us
    another operation x6, other arithmetic, shards(): lower_factor = jnp.linalg.cholesky(gram_total)  34 us
    psum x1, waiting for transfers between devices, shards(): lax.psum(lax.psum(local_gram, 'lo'), 'hi') * (1.0 / (count_here * devices))  33.8 us
    another operation x4, other arithmetic, shards(): lax.linalg.triangular_solve(lower_factor, current, left_side=False, lower...  22.1 us
    another operation x3, matrix products, shards(): lax.linalg.triangular_solve(lower_factor, current, left_side=False, lower...  9.15 us
    all_to_all x1, blocking collectives, shards(): lax.all_to_all(outgoing, 'lo', split_axis=0, concat_axis=0, tiled=True)  8.94 us
  transfers between devices with their start and end apart: 3, of which 3 were waited for; matrix products, arithmetic and copies ran while one was open for 0% of the time, Pallas kernels for 0%

profile of v1, /device:TPU:0, one launch (start us, length us, event | category | flops | bytes accessed | tf_op | source)
XLA Modules:
  0.0 412.0 jit_solution(12736564312410361710)
XLA Ops:
  7.2 0.9 dynamic-update-slice.11
  8.1 42.0 %all-reduce.1 = s32[512]{0:T(512)S(1)} all-reduce(s32[512]{0:T(512)S(1)} %dynamic-update-slice.11), channel_id=1, replica_groups=mesh['hi'=4,'lo'=8] {'hi','lo'}, use_global_device_ids=true, to_apply=%add.1 | all-reduce | flops 512 | bytes 4096
  50.1 0.8 broadcast_multiply_fusion.6
  50.9 0.1 mul.371
  51.0 0.8 broadcast_multiply_fusion.5
  51.7 0.1 mul.375
  51.8 0.7 convert_element_type.16
  52.6 0.8 broadcast_multiply_fusion.4
  53.4 0.8 broadcast_multiply_fusion.3
  54.2 0.1 mul.383
  54.3 0.9 broadcast_multiply_fusion.1
  55.2 0.2 dynamic-slice_reduce_fusion
  55.5 0.1 mul.427
  55.6 0.7 reshape.344
  56.2 2.6 broadcast_multiply_fusion
  58.8 6.3 %fusion.2 = f32[64,64,256]{2,0,1:T(8,128)S(1)} fusion(f32[64,64,1]{1,0,2:T(8,128)S(1)} %reshape.344, f32[64,64,256]{2,1,0:T(8,128)S(1)} %bitcast.55), kind=kOutput, calls=%fused_computation.7 | convolution fusion | flops 805306368 | bytes 8404992 | tf_op jit(solution)/shard_map/ab,bcp->acp/dot_general | solution.py:35
  65.1 7.0 %fusion = f32[64,256,64]{1,2,0:T(8,128)} fusion(f32[64,64,1]{1,0,2:T(8,128)S(1)} %reshape.344, f32[64,64,256]{2,0,1:T(8,128)S(1)} %fusion.2), kind=kOutput, calls=%fused_computation.5 | convolution fusion | flops 805306368 | bytes 8404992 | tf_op jit(solution)/shard_map/cd,adp->acp/dot_general | solution.py:36
  72.1 3.8 gather_fusion
  75.9 1.0 select_multiply_fusion
  77.1 0.2 select_reduce_fusion.2
  77.3 135.4 %reduce-scatter.2.cloned.1.call-done = f32[16,256]{1,0:T(8,128)} async-done(((f32[512,256]{1,0:T(8,128)}), f32[16,256]{1,0:T(8,128)}) %reduce-scatter.2.cloned.1.call-update) | async-done | bytes 16400 | tf_op jit(solution)/shard_map/reduce_scatter | solution.py:43
  212.7 0.8 fusion.14
  213.6 8.9 %all_to_all.5 = f32[8,2,256]{2,1,0:T(2,128)S(1)} all-to-all(f32[8,2,256]{2,1,0:T(2,128)S(1)} %copy.33), channel_id=1, replica_groups=mesh['hi'=4,'lo'=8] {'lo'}, dimensions={0} | all-to-all | bytes 32768 | tf_op jit(solution)/shard_map/all_to_all | solution.py:54
  222.6 1.1 convolution_bitcast_fusion
  223.7 67.5 %all-reduce.5.cloned.1.call-done = f32[256,256]{0,1:T(8,128)} async-done(((f32[256,256]{0,1:T(8,128)}), f32[256,256]{0,1:T(8,128)}) %all-reduce.5.cloned.1.call-update) | async-done | bytes 262160 | tf_op jit(solution)/shard_map/psum | solution.py:58
  291.3 33.8 %all-reduce.7.cloned.1.call-done = f32[256,256]{0,1:T(8,128)} async-done(((f32[256,256]{0,1:T(8,128)}), f32[256,256]{0,1:T(8,128)}) %all-reduce.7.cloned.1.call-update) | async-done | bytes 262160 | tf_op jit(solution)/shard_map/psum | solution.py:58
  325.1 1.0 broadcast_multiply_fusion.2
  326.0 0.1 copy.37
  326.2 1.0 fusion.6
  327.2 11.7 %cholesky.50 = f32[128,128]{1,0:T(8,128)S(1)} custom-call(f32[128,128]{1,0:T(8,128)S(1)} %cholesky.118), custom_call_target="Cholesky" | custom-call | tf_op jit(solution)/shard_map/jit(cholesky)/cholesky | solution.py:59
  338.9 9.8 %custom-call.14 = f32[1,128,128]{1,2,0:T(8,128)S(1)} custom-call(f32[1,128,128]{2,1,0:T(8,128)S(1)} %get-tuple-element.38), custom_call_target="InvertDiagBlocksLowerTriangular" | custom-call | tf_op jit(solution)/shard_map/jit(cholesky)/cholesky | solution.py:59
  348.8 0.2 constant_dynamic-update-slice_fusion.1
  349.0 0.3 convolution_subtract_fusion.1
  349.3 11.7 %cholesky.105 = f32[128,128]{1,0:T(8,128)S(1)} custom-call(f32[128,128]{1,0:T(8,128)S(1)} %convolution_subtract_fusion.1), custom_call_target="Cholesky" | custom-call | tf_op jit(solution)/shard_map/jit(cholesky)/cholesky | solution.py:59
  361.0 0.6 compare_reduce_fusion
  363.0 0.8 copy.38
  363.9 4.1 while.1
  363.9 0.6 fusion.32
  364.5 1.4 bitcast_dynamic-update-slice_fusion.2
  366.0 0.6 fusion.32
  366.6 1.4 bitcast_dynamic-update-slice_fusion.2
  368.0 19.7 %custom-call.15 = f32[2,128,128]{1,2,0:T(8,128)S(1)} custom-call(f32[2,128,128]{2,1,0:T(8,128)S(1)} %get-tuple-element.10), custom_call_target="InvertDiagBlocksLowerTriangular" | custom-call | tf_op jit(solution)/shard_map/triangular_solve | solution.py:60
  387.7 3.7 fusion.4
  391.4 3.4 convolution_subtract_fusion
  394.8 2.0 fusion.9
  396.9 2.4 pad_maximum_fusion
  399.3 5.6 %copy.39 = f32[4096,256]{1,0:T(8,128)} copy(f32[4096,256]{0,1:T(8,128)} %pad_maximum_fusion) | data formatting | bytes 8388608
  404.9 0.6 copy.63
  (31 shorter events, 0.7 us)
Async XLA Ops:
  7.2 205.6 %reduce-scatter.2.cloned.1.call-start = ((), (), s32[]{:S(2)}) async-start(), calls=%async_computation.2 | async-start | bytes 540672 | tf_op jit(solution)/shard_map/reduce_scatter | solution.py:43
  72.1 4.9 %copy-start.1 = (s32[16,1]{0,1:T(1,128)S(1)}, s32[16,1]{0,1:T(1,128)}, u32[]{:S(2)}) copy-start(s32[16,1]{0,1:T(1,128)} %param.10) | copy-start | bytes 196
  76.9 214.3 %all-reduce.5.cloned.1.call-start = ((), (), s32[]{:S(2)}) async-start(), calls=%async_computation.3 | async-start | bytes 524288 | tf_op jit(solution)/shard_map/psum | solution.py:58
  223.7 101.4 %all-reduce.7.cloned.1.call-start = ((), (), s32[]{:S(2)}) async-start(), calls=%async_computation.4 | async-start | bytes 524288 | tf_op jit(solution)/shard_map/psum | solution.py:58
  387.7 3.7 copy-start
Sparse Core Ops, SparseCore 0:
  77.1 135.6 reduce-scatter.1
  223.8 67.3 all-reduce.4
  293.6 31.4 all-reduce.6
